TPU v7x, 128 devices: a whole 4x4x4 slice. The times are simulated.
128 devices in a mesh: req: 4 (over z), tile: 8 (over y, core), span: 4 (over x).
Axes of the slice: x: 4, y: 4, z: 4, core: 2. Of those that a mesh axis runs over, the one named last changes fastest.
Arguments:
- latents: bfloat16 [32, 64, 128, 512], P(('req', 'span'), 'tile'), may hold values from -12 to 12
- frame_counts: int32 [4], replicated, may hold values from 1 to 16, 32 in all
- norm_gain: float32 [512], replicated, may hold values from 0.1 to 1.9
- norm_shift: float32 [512], replicated, may hold values from -3 to 3
- conv_weight: bfloat16 [3, 3, 3, 512, 512], replicated, may hold values from -0.0546875 to 0.0546875
- conv_bias: float32 [512], replicated, may hold values from -2 to 2
Outputs:
- decoded: bfloat16 [32, 64, 128, 512], P(('req', 'span'), 'tile')
Inputs may be any that keep to these rules, and one draw needn't show every extreme that they name: `frame_counts`: the 4 counts sum to 32, and the largest is exactly 16.
All inputs are finite; a program needn't handle non-finite values.
Results may differ from a plain program's by a relative error of at most 0.0031.
Values may be sent and summed in bfloat16 or wider, within the bound.
No kernel may reach another device: no remote copies, remote signals or barrier semaphores. Data moves between devices by JAX's collectives and lax.ppermute only.
A program may use at most 192 MiB of HBM per device.

v0:
```python
import functools

import jax
import jax.numpy as jnp
from jax import lax
from jax.experimental import pallas as pl
from jax.experimental.pallas import tpu as pltpu
from jax.sharding import PartitionSpec as P

GROUPS = 32
EPSILON = 1e-06
EARLY = 5
LANES = 128
HIGHEST = lax.Precision.HIGHEST


def layout(counts, place, frames):
    ends = [counts[0]]
    for r in range(1, 3):
        ends.append(ends[-1] + counts[r])
    first = place[0] * frames

    def request_of(position):
        request = 0
        for end in ends:
            request += (position >= end).astype(jnp.int32)
        return request

    def start_of(position):
        start = 0
        for end in ends:
            start = jnp.where(position >= end, end, start)
        return start

    def request(k):
        return request_of(jnp.maximum(first - 2 + k, 0))

    def source(output, tap):
        position = first + output
        return jnp.maximum(position - 2 + tap, start_of(position)) - first + 2

    return request, source


def group_matrix(channels, per_group, transpose):
    shape = (LANES, channels) if transpose else (channels, LANES)
    lane = lax.broadcasted_iota(jnp.int32, shape, 0 if transpose else 1)
    channel = lax.broadcasted_iota(jnp.int32, shape, 1 if transpose else 0)
    return (channel // per_group == lane).astype(jnp.float32)


def stats_kernel(per_group, frames, counts, place, x_ref, out_ref):
    frame = pl.program_id(0)
    rows, cols, channels = x_ref.shape[1:]

    def one_row(i, carry):
        total, squares = carry
        v = x_ref[0, i].astype(jnp.float32).reshape(cols // 8, 8, channels)
        return total + jnp.sum(v, axis=0), squares + jnp.sum(v * v, axis=0)

    zero = jnp.zeros((8, channels), jnp.float32)
    total, squares = lax.fori_loop(0, rows, one_row, (zero, zero))
    members = group_matrix(channels, per_group, False)
    grouped = [
        jnp.sum(
            lax.dot(part, members, precision=HIGHEST, preferred_element_type=jnp.float32),
            axis=0,
            keepdims=True,
        )
        for part in (total, squares)
    ]
    row = lax.broadcasted_iota(jnp.int32, (8, LANES), 0)
    request = layout(counts, place, frames)[0](2 + frame)
    mine = jnp.where(row == request, grouped[0], 0.0) + jnp.where(
        row == request + 4, grouped[1], 0.0
    )

    @pl.when(frame == 0)
    def _():
        out_ref[...] = mine

    @pl.when(frame != 0)
    def _():
        out_ref[...] += mine


def local_stats(counts, place, latents, per_group):
    frames, rows, cols, channels = latents.shape
    return pl.pallas_call(
        functools.partial(stats_kernel, per_group, frames),
        grid_spec=pltpu.PrefetchScalarGridSpec(
            num_scalar_prefetch=2,
            grid=(frames,),
            in_specs=[pl.BlockSpec((1, rows, cols, channels), lambda f, *_: (f, 0, 0, 0))],
            out_specs=pl.BlockSpec((8, LANES), lambda f, *_: (0, 0)),
        ),
        out_shape=jax.ShapeDtypeStruct((8, LANES), jnp.float32),
        name="local_stats",
    )(counts, place, latents)


def affine_of(counts, total, gain, shift, cells_per_frame, per_group):
    channels = gain.shape[1]
    row = lax.broadcasted_iota(jnp.int32, (4, LANES), 0)
    frames = jnp.zeros((4, LANES), jnp.float32)
    for r in range(4):
        frames = jnp.where(row == r, counts[r].astype(jnp.float32), frames)
    cells = frames * float(cells_per_frame)
    mean = total[0:4] / cells
    scale = lax.rsqrt(total[4:8] / cells - mean * mean + EPSILON)
    spread = group_matrix(channels, per_group, True)
    both = lax.dot(
        jnp.concatenate([mean, scale], axis=0),
        spread,
        precision=HIGHEST,
        preferred_element_type=jnp.float32,
    )
    factor = both[4:8] * gain
    return jnp.concatenate([factor, shift - both[0:4] * factor], axis=0)


def normalize_rows(raw, stacked, slot, rows, factor, term):
    cols, channels = raw.shape[2:]
    place = lax.broadcasted_iota(jnp.int32, (cols, LANES), 0)
    for i in rows:
        for at in range(0, channels, LANES):
            lanes = slice(at, at + LANES)
            u = raw[slot, i, :, lanes].astype(jnp.float32) * factor[:, lanes] + term[:, lanes]
            h = u * jnp.tanh(u) + u
            left = jnp.where(place == 0, h, pltpu.roll(h, 1, 0))
            right = jnp.where(place == cols - 1, h, pltpu.roll(h, cols - 1, 0))
            for tap, value in enumerate((left, h, right)):
                begin = tap * channels + at
                stacked[slot, i, :, begin : begin + LANES] = value.astype(jnp.bfloat16)


def conv_kernel(stage, cells_per_frame, per_group, *refs):
    refs = list(refs)
    take = lambda n: [refs.pop(0) for _ in range(n)]
    counts, place = take(2)
    lat, top, bottom = take(3)
    if stage != "a":
        near_rows, pair_rows, inner_1 = take(3)
    if stage == "c":
        far_rows, inner_0 = take(2)
    (weight,) = take(1)
    if stage == "a":
        total_ref, gain_ref, shift_ref = take(3)
        affine_out, acc_out = take(2)
    elif stage == "b":
        affine_in, bias_ref, acc_in = take(3)
        acc_out, decoded = take(2)
    else:
        affine_in, bias_ref, acc_in, _ = take(4)
        (decoded,) = take(1)
    raw, stacked, kernels, acc, affine, held, residual, io_sem, w_sem, out_sem = refs
    rows, cols, channels = lat.shape[1:]
    request_of, source_of = layout(counts, place, lat.shape[0])
    tile = place[1]

    if stage == "a":
        sources = [2, 3]
        local_only = True
        second = source_of(1, 1) - 2
        plan = [(0, 2, 0), (1, 2, 1), (1, 1, second)]
    elif stage == "b":
        sources = [source_of(1, 0), source_of(0, 1)]
        local_only = False
        plan = [(1, 0, 0), (0, 1, 1)]
    else:
        sources = [source_of(0, 0)]
        local_only = False
        plan = [(0, 0, 0)]

    is_top = tile == 0
    is_bottom = tile == place[2] - 1
    first_core = lax.rem(tile, 2) == 0

    def copy(src, dst, sem):
        return pltpu.make_async_copy(src, dst, sem)

    def pick(cond, yes, no):
        @pl.when(cond)
        def _():
            yes()

        @pl.when(jnp.logical_not(cond))
        def _():
            no()

    def load(slot, frame):
        upper, lower = raw.at[slot, 0], raw.at[slot, rows + 1]
        sems = [io_sem.at[slot, k] for k in range(4)]

        def from_local():
            k = frame - 2
            copy(lat.at[k, pl.ds(0, rows - 1)], raw.at[slot, pl.ds(1, rows - 1)], sems[0]).start()
            copy(lat.at[k, rows - 1], raw.at[slot, rows], sems[3]).start()
            pick(
                is_top,
                lambda: copy(lat.at[k, 0], upper, sems[1]).start(),
                lambda: copy(top.at[k], upper, sems[1]).start(),
            )
            pick(
                is_bottom,
                lambda: copy(lat.at[k, rows - 1], lower, sems[2]).start(),
                lambda: copy(bottom.at[k], lower, sems[2]).start(),
            )

        def from_remote():
            early = near_rows.shape[0]
            late = rows - early

            def frame_one():
                def first():
                    copy(near_rows, raw.at[slot, pl.ds(late + 1, early)], sems[0]).start()
                    copy(
                        pair_rows.at[pl.ds(2, late - 1)], raw.at[slot, pl.ds(2, late - 1)], sems[0]
                    ).start()
                    copy(pair_rows.at[1], raw.at[slot, 1], sems[3]).start()
                    pick(
                        is_top,
                        lambda: copy(pair_rows.at[1], upper, sems[1]).start(),
                        lambda: copy(pair_rows.at[0], upper, sems[1]).start(),
                    )
                    copy(inner_1.at[0], lower, sems[2]).start()

                def second():
                    copy(near_rows, raw.at[slot, pl.ds(1, early)], sems[0]).start()
                    copy(
                        pair_rows.at[pl.ds(0, late - 1)],
                        raw.at[slot, pl.ds(early + 1, late - 1)],
                        sems[0],
                    ).start()
                    copy(pair_rows.at[late - 1], raw.at[slot, rows], sems[3]).start()
                    pick(
                        is_bottom,
                        lambda: copy(pair_rows.at[late - 1], lower, sems[1]).start(),
                        lambda: copy(pair_rows.at[late], lower, sems[1]).start(),
                    )
                    copy(inner_1.at[0], upper, sems[2]).start()

                pick(first_core, first, second)

            def frame_zero():
                def first():
                    copy(far_rows, raw.at[slot, pl.ds(1, rows - 1)], sems[0]).start()
                    copy(pair_rows.at[late + 2], raw.at[slot, rows], sems[3]).start()
                    pick(
                        is_top,
                        lambda: copy(far_rows.at[0], upper, sems[1]).start(),
                        lambda: copy(pair_rows.at[late + 1], upper, sems[1]).start(),
                    )
                    copy(inner_0.at[0], lower, sems[2]).start()

                def second():
                    copy(far_rows, raw.at[slot, pl.ds(2, rows - 1)], sems[0]).start()
                    copy(pair_rows.at[late + 2], raw.at[slot, 1], sems[3]).start()
                    pick(
                        is_bottom,
                        lambda: copy(far_rows.at[rows - 2], lower, sems[1]).start(),
                        lambda: copy(pair_rows.at[late + 1], lower, sems[1]).start(),
                    )
                    copy(inner_0.at[0], upper, sems[2]).start()

                pick(first_core, first, second)

            if stage == "b":
                frame_one()
            else:
                pick(frame == 1, frame_one, frame_zero)

        if local_only:
            from_local()
        else:
            pick(frame >= 2, from_local, from_remote)

    def loaded(slot):
        copy(
            lat.at[0, pl.ds(0, rows - 1)], raw.at[slot, pl.ds(1, rows - 1)], io_sem.at[slot, 0]
        ).wait()
        for k, place in ((1, 0), (2, rows + 1), (3, rows)):
            copy(lat.at[0, 0], raw.at[slot, place], io_sem.at[slot, k]).wait()

    upper_rows = rows // 2
    pieces, order, done = [], [], []
    for o, a, slot in plan:
        if any(later[0] == o for later in plan[len(done) + 1 :]):
            order += [(o, a, slot, half, b) for b in range(3) for half in range(2)]
        else:
            order += [(o, a, slot, half, b) for half in range(2) for b in range(3)]
        done.append(o)
        pieces += [(a, b) for b in range(3) if (a, b) not in pieces]
    loads = [
        copy(weight.at[a, b], kernels.at[k], w_sem.at[k])
        for k, (a, b) in enumerate(pieces)
    ]
    sent = 0

    def send_until(n):
        nonlocal sent
        while sent < min(n, len(loads)):
            loads[sent].start()
            sent += 1

    load(0, sources[0])
    send_until(1)
    if stage == "a":
        affine[...] = affine_of(
            counts, total_ref[...], gain_ref[...], shift_ref[...], cells_per_frame, per_group
        )
        affine_out[...] = affine[...]
    else:
        affine[...] = affine_in[...]

    def params(frame):
        request = request_of(frame)
        factor = affine[pl.ds(request, 1), :] * 0.5
        term = affine[pl.ds(request + 4, 1), :] * 0.5
        return factor, term

    loaded(0)
    if len(sources) > 1:
        load(1, sources[1])
    send_until(2)
    begun = params(sources[0])
    normalize_rows(raw, stacked, 0, range(rows - 2), *begun)

    def held_copy(o):
        return copy(acc_in.at[o], held.at[o], io_sem.at[o, 4])

    def finish(o, half):
        if half == 0:
            held_copy(o).wait()
            copy(lat.at[0], residual, out_sem.at[rows]).wait()
        for i in range(upper_rows):
            r = half * upper_rows + i
            cell = slice(i * cols, (i + 1) * cols)
            value = residual[r].astype(jnp.float32) + (
                acc[o, half, cell] + held[o, half, cell] + bias_ref[...]
            )
            residual[r] = value.astype(jnp.bfloat16)
            sends.append(copy(residual.at[r], decoded.at[o, r], out_sem.at[r]))
            sends[-1].start()

    sends, pending = [], []
    waited = set()
    seen = set()
    for step, (o, a, slot, half, b) in enumerate(order):
        ahead = 2 <= step < 6 and len(sources) > 1
        if step == 2 and ahead:
            loaded(1)
            factor, term = params(sources[1])
        k = pieces.index((a, b))
        if k not in waited:
            loads[k].wait()
            waited.add(k)
            send_until(k + 3)
        if step == 0 and stage != "a":
            for n in sorted({o for o, *_ in plan}, reverse=True):
                held_copy(n).start()
            copy(lat.at[1 if stage == "b" else 0], residual, out_sem.at[rows]).start()
        finished = stage == "c" or (stage == "b" and o == 1)
        top_row = half * upper_rows + b
        part = jnp.dot(
            stacked[slot, top_row : top_row + upper_rows].reshape(upper_rows * cols, 3 * channels),
            kernels[k],
            preferred_element_type=jnp.float32,
        )
        if stage != "a" and not finished and b == 2:
            if half == 0:
                held_copy(o).wait()
            part = part + held[o, half]
        if (o, half) in seen:
            acc[o, half] += part
        else:
            acc[o, half] = part
            seen.add((o, half))
        if step < 2:
            normalize_rows(raw, stacked, 0, range(rows - 2 + 2 * step, rows + 2 * step), *begun)
        if ahead:
            turn = range(3 * (step - 2), min(3 * (step - 2) + 3, rows + 2))
            normalize_rows(raw, stacked, 1, turn, factor, term)
        last = not any(x[0] == o and x[3] == half for x in order[step + 1 :])
        if last and finished:
            pending.append((step + 2, o, half))
        elif last:
            sends.append(copy(acc.at[o, half], acc_out.at[o, half], io_sem.at[half, 5 + o]))
            sends[-1].start()
        while pending and (pending[0][0] <= step or step == len(order) - 1):
            finish(*pending.pop(0)[1:])
    for c in sends:
        c.wait()


def conv_stage(stage, counts, place, latents, extras, weight, small, acc=None, decoded=None, per_group=16, cells_per_frame=0):
    _, rows, cols, channels = latents.shape
    any_spec = pl.BlockSpec(memory_space=pl.ANY)
    vmem = pl.BlockSpec(memory_space=pltpu.VMEM)
    args = [counts, place, latents, *extras, weight, *small]
    specs = [pl.BlockSpec(memory_space=pltpu.SMEM)] * 2 + [any_spec] * (2 + len(extras)) + [vmem] * len(small)
    aliases = {}
    if acc is not None:
        args.append(acc)
        specs.append(any_spec)
    acc_shape = lambda n: jax.ShapeDtypeStruct((n, 2, rows * cols // 2, channels), jnp.float32)
    out_shape = jax.ShapeDtypeStruct(latents.shape, jnp.bfloat16)
    if stage == "a":
        outs = (jax.ShapeDtypeStruct((8, channels), jnp.float32), acc_shape(2))
        out_specs = (vmem, any_spec)
        slots, blocks, held = 2, 6, 2
    elif stage == "b":
        outs = (acc_shape(1), out_shape)
        out_specs = (any_spec, any_spec)
        slots, blocks, held = 2, 6, 2
    else:
        aliases = {len(args): 0}
        args.append(decoded)
        specs.append(any_spec)
        outs = out_shape
        out_specs = any_spec
        slots, blocks, held = 1, 3, 1
    return pl.pallas_call(
        functools.partial(conv_kernel, stage, cells_per_frame, per_group),
        in_specs=specs,
        out_specs=out_specs,
        out_shape=outs,
        input_output_aliases=aliases,
        scratch_shapes=[
            pltpu.VMEM((slots, rows + 2, cols, channels), jnp.bfloat16),
            pltpu.VMEM((slots, rows + 2, cols, 3 * channels), jnp.bfloat16),
            pltpu.VMEM((blocks, 3 * channels, channels), jnp.bfloat16),
            pltpu.VMEM((held, 2, rows * cols // 2, channels), jnp.float32),
            pltpu.VMEM((8, channels), jnp.float32),
            pltpu.VMEM((held, 2, rows * cols // 2, channels), jnp.float32),
            pltpu.VMEM((rows, cols, channels), jnp.bfloat16),
            pltpu.SemaphoreType.DMA((2, 7)),
            pltpu.SemaphoreType.DMA((blocks,)),
            pltpu.SemaphoreType.DMA((rows + 1,)),
        ],
        compiler_params=pltpu.CompilerParams(vmem_limit_bytes=58 << 20),
    )(*args)


def shards(latents, frame_counts, norm_gain, norm_shift, conv_weight, conv_bias):
    _, rows, cols, channels = latents.shape
    per_group = channels // GROUPS
    spread = ("req", "span")
    tile = lax.axis_index("tile")
    place = jnp.stack([lax.axis_index(spread), tile, lax.axis_size("tile")]).astype(jnp.int32)

    onward = [(i, i + 1) for i in range(lax.axis_size("req") * lax.axis_size("span") - 1)]
    count = lax.axis_size("tile")
    down = [(i, i + 1) for i in range(count - 1)]
    up = [(i + 1, i) for i in range(count - 1)]
    swap = [(i, i ^ 1) for i in range(count)]
    core = tile % 2
    first_core = core == 0

    def after(value, *others):
        return lax.optimization_barrier((value, *others))[0]

    def fold(value, axis, partner):
        return value + lax.ppermute(value, axis, partner)

    ring = lambda step: [(i, i ^ 1 if step == 0 else 3 - i) for i in range(4)]
    rung = lambda step: [
        (i, 2 * (i // 2 ^ 1 if step == 0 else 3 - i // 2) + i % 2) for i in range(count)
    ]

    late = rows - EARLY
    near_send = lax.dynamic_slice_in_dim(latents[1], late * (1 - core), EARLY, axis=0)
    near_rows = lax.ppermute(near_send, spread, onward)
    total = local_stats(frame_counts, place, latents, per_group)
    total = fold(total, "tile", swap)
    total = fold(total, "tile", rung(0))
    total = fold(total, "tile", rung(1))
    top = lax.ppermute(after(latents[:, -1], total), "tile", down)
    total = fold(total, "req", ring(0))
    bottom = lax.ppermute(after(latents[:, 0], total), "tile", up)
    total = fold(total, "req", ring(1))
    other = lax.ppermute(total, "span", ring(0))
    pair_send = jnp.where(
        first_core,
        jnp.concatenate([top[1:], latents[1, :late], top[:1], latents[0, rows - 1 :]]),
        jnp.concatenate([latents[1, EARLY:], bottom[1:], bottom[:1], latents[0, :1]]),
    )
    far_send = lax.dynamic_slice_in_dim(latents[0], core, rows - 1, axis=0)
    total = total + other
    near_rows, total = lax.optimization_barrier((near_rows, total))
    inner_send = jnp.where(first_core, near_rows[EARLY - 1], near_rows[0])[None]
    inner_1 = lax.ppermute(inner_send, "tile", swap)
    other = lax.ppermute(total, "span", ring(1))
    pair_rows = lax.ppermute(pair_send, spread, onward)
    far_rows = lax.ppermute(far_send, spread, onward)
    total = total + other

    cells_per_frame = rows * count * cols * per_group
    weight = conv_weight.reshape(3, 3, 3 * channels, channels)
    gain, shift, bias = (v.reshape(1, channels) for v in (norm_gain, norm_shift, conv_bias))
    run = functools.partial(conv_stage, per_group=per_group, cells_per_frame=cells_per_frame)
    near = (top, bottom)
    middle = (top, bottom, near_rows, pair_rows, inner_1)
    affine, acc = run("a", frame_counts, place, latents, near, weight, (total, gain, shift))
    pair_rows, acc = lax.optimization_barrier((pair_rows, acc))
    inner_0 = lax.ppermute(pair_rows[late + 2 :], "tile", swap)
    acc, decoded = run("b", frame_counts, place, latents, middle[:3] + (pair_rows, inner_1), weight, (affine, bias), acc)
    far = (top, bottom, near_rows, pair_rows, inner_1, far_rows, inner_0)
    return run("c", frame_counts, place, latents, far, weight, (affine, bias), acc, decoded)


def solution(mesh):
    placed = (P(("req", "span"), "tile", None, None), P(), P(), P(), P(), P())
    return jax.shard_map(
        shards,
        mesh=mesh,
        in_specs=placed,
        out_specs=P(("req", "span"), "tile", None, None),
        check_vma=False,
    )
```

profile of v0, /device:TPU:23, one launch (start us, length us, event | category | flops | bytes accessed | tf_op | source)
XLA Modules:
  0.0 124.4 jit_solution(15706223054157513026)
XLA Ops:
  0.0 0.6 pad_add_fusion.place.refs_1_
  0.6 3.8 %local_stats.1 = f32[8,128]{1,0:T(8,128)} custom-call(s32[4]{0:T(128)} %refs_0_.5, s32[3]{0:T(128)} %pad_add_fusion.place.refs_1_, bf16[2,8,128,512]{3,2,1,0:T(8,128)(2,1)} %refs_2_.5), custom_call_target="tpu_custom_call" | custom-call | tf_op jit(solution)/shard_map/local_stats/pallas_call | solution.py:89
  4.4 0.7 collective-permute-start
  5.1 1.2 fusion
  6.3 1.1 collective-permute-start.1
  7.4 0.9 dynamic-slice_bitcast_fusion.1
  8.3 3.4 %collective-permute-start.6 = (bf16[5,128,512]{2,1,0:T(8,128)(2,1)}, bf16[5,128,512]{2,1,0:T(8,128)(2,1)S(1)}, u32[]{:S(2)}, u32[]{:S(2)}) collective-permute-start(bf16[5,128,512]{2,1,0:T(8,128)(2,1)} %dynamic-slice_bitcast_fusion.1), channel_id=1, source_target_pairs={{0,1},{1,2},{2,3},{3,32},{32,33},{33,34},{34,35},{35,64},{64,65},{... | collective-permute-start | bytes 1966088 | tf_op jit(solution)/shard_map/ppermute | solution.py:473
  11.8 0.8 slice_bitcast_fusion.2
  12.7 1.9 %collective-permute-done.2 = f32[8,128]{1,0:T(8,128)S(1)} collective-permute-done((f32[8,128]{1,0:T(8,128)S(1)}, f32[8,128]{1,0:T(8,128)S(1)}, u32[]{:S(2)}, u32[]{:S(2)}) %collective-permute-start.2) | collective-permute-done | bytes 4128 | tf_op jit(solution)/shard_map/ppermute | solution.py:464
  14.6 1.6 %collective-permute-start.4 = (f32[8,128]{1,0:T(8,128)S(1)}, f32[8,128]{1,0:T(8,128)S(1)}, u32[]{:S(2)}, u32[]{:S(2)}) collective-permute-start(f32[8,128]{1,0:T(8,128)S(1)} %add.37), channel_id=1, source_target_pairs={{0,32},{32,0},{64,96},{96,64},{1,33},{33,1},{65,97},{97,65},{2,34}... | collective-permute-start | bytes 12296 | tf_op jit(solution)/shard_map/ppermute | solution.py:464
  16.2 5.3 %collective-permute-start.3 = (bf16[2,128,512]{2,1,0:T(8,128)(2,1)}, bf16[2,128,512]{2,1,0:T(8,128)(2,1)S(1)}, u32[]{:S(2)}, u32[]{:S(2)}) collective-permute-start(bf16[2,128,512]{2,1,0:T(8,128)(2,1)} %get-tuple-element.15), channel_id=1, source_target_pairs={{0,4},{4,8},{8,12},{12,16},{16,20},{20,24},{24,28},{1,5},{5,9},{9,... | collective-permute-start | bytes 786440 | tf_op jit(solution)/shard_map/ppermute | solution.py:478
  21.5 1.0 slice_bitcast_fusion
  22.5 1.9 %collective-permute-start.5 = (bf16[2,128,512]{2,1,0:T(8,128)(2,1)}, bf16[2,128,512]{2,1,0:T(8,128)(2,1)S(1)}, u32[]{:S(2)}, u32[]{:S(2)}) collective-permute-start(bf16[2,128,512]{2,1,0:T(8,128)(2,1)} %get-tuple-element.16), channel_id=1, source_target_pairs={{4,0},{8,4},{12,8},{16,12},{20,16},{24,20},{28,24},{5,1},{9,5},{13... | collective-permute-start | bytes 786440 | tf_op jit(solution)/shard_map/ppermute | solution.py:480
  24.4 0.7 collective-permute-done.3.refs_3_
  25.1 5.2 %collective-permute-done.5.refs_4_ = bf16[2,128,512]{2,1,0:T(8,128)(2,1)S(1)} collective-permute-done((bf16[2,128,512]{2,1,0:T(8,128)(2,1)}, bf16[2,128,512]{2,1,0:T(8,128)(2,1)S(1)}, u32[]{:S(2)}, u32[]{:S(2)}) %collective-permute-start.5) | collective-permute-done | bytes 262176 | tf_op jit(solution)/shard_map/ppermute | solution.py:480
  30.4 1.4 %maximum_select_fusion = bf16[6,128,512]{2,1,0:T(8,128)(2,1)S(1)} fusion(bf16[1,128,512]{2,1,0:T(8,128)(2,1)S(1)} %get-tuple-element.30, bf16[1,128,512]{2,1,0:T(8,128)(2,1)S(1)} %get-tuple-element.36, bf16[3,128,512]{2,1,0:T(8,128)(2,1)} %get-tuple-element.28, bf16[1,128,512]{2,1,0:T(8,128)(2,1)S(1)} %get-tuple-element.35, ...), kind=kLoop, calls=%fused_computation.1 | loop fusion | flops 2752512 | bytes 2359297 | tf_op jit(solution)/shard_map/jit(_where)/select_n | solution.py:483
  31.8 1.9 %collective-permute-start.9 = (bf16[6,128,512]{2,1,0:T(8,128)(2,1)S(1)}, bf16[6,128,512]{2,1,0:T(8,128)(2,1)S(1)}, u32[]{:S(2)}, u32[]{:S(2)}) collective-permute-start(bf16[6,128,512]{2,1,0:T(8,128)(2,1)S(1)} %maximum_select_fusion), channel_id=1, source_target_pairs={{0,1},{1,2},{2,3},{3,32},{32,33},{33,34},{34,35},{35,64},{64,65},{... | collective-permute-start | bytes 2359304 | tf_op jit(solution)/shard_map/ppermute | solution.py:494
  33.7 1.3 %dynamic-slice_bitcast_fusion = bf16[7,128,512]{2,1,0:T(8,128)(2,1)S(1)} fusion(bf16[1,8,128,512]{3,2,1,0:T(8,128)(2,1)} %get-tuple-element.25, s32[]{:T(128)S(6)} %select_n.36), kind=kLoop, calls=%fused_computation | loop fusion | bytes 1835012 | tf_op jit(solution)/shard_map/dynamic_slice | solution.py:488
  35.0 2.5 %collective-permute-start.12 = (bf16[7,128,512]{2,1,0:T(8,128)(2,1)S(1)}, bf16[7,128,512]{2,1,0:T(8,128)(2,1)S(1)}, u32[]{:S(2)}, u32[]{:S(2)}) collective-permute-start(bf16[7,128,512]{2,1,0:T(8,128)(2,1)S(1)} %dynamic-slice_bitcast_fusion), channel_id=1, source_target_pairs={{0,1},{1,2},{2,3},{3,32},{32,33},{33,34},{34,35},{35,64},{64,65},{... | collective-permute-start | bytes 2752520 | tf_op jit(solution)/shard_map/ppermute | solution.py:495
  37.5 0.2 collective-permute-start.7
  37.7 3.6 %collective-permute-done.7 = f32[8,128]{1,0:T(8,128)S(1)} collective-permute-done((f32[8,128]{1,0:T(8,128)S(1)}, f32[8,128]{1,0:T(8,128)S(1)}, u32[]{:S(2)}, u32[]{:S(2)}) %collective-permute-start.7) | collective-permute-done | bytes 4128 | tf_op jit(solution)/shard_map/ppermute | solution.py:464
  41.3 0.9 collective-permute-start.8
  42.2 29.4 %collective-permute-done.8 = f32[8,128]{1,0:T(8,128)S(1)} collective-permute-done((f32[8,128]{1,0:T(8,128)S(1)}, f32[8,128]{1,0:T(8,128)S(1)}, u32[]{:S(2)}, u32[]{:S(2)}) %collective-permute-start.8) | collective-permute-done | bytes 4128 | tf_op jit(solution)/shard_map/ppermute | solution.py:482
  71.7 0.3 collective-permute-start.11
  72.0 3.7 %collective-permute-done.10 = f32[8,128]{1,0:T(8,128)S(1)} collective-permute-done((f32[8,128]{1,0:T(8,128)S(1)}, f32[8,128]{1,0:T(8,128)S(1)}, u32[]{:S(2)}, u32[]{:S(2)}) %collective-permute-start.10) | collective-permute-done | bytes 4128 | tf_op jit(solution)/shard_map/ppermute | solution.py:493
  75.6 0.6 add.43.refs_6_
  76.2 20.5 %shard_map.64 = (f32[8,512]{1,0:T(8,128)}, f32[2,2,512,512]{3,2,1,0:T(8,128)}) custom-call(s32[4]{0:T(128)} %refs_0_.5, s32[3]{0:T(128)} %pad_add_fusion.place.refs_1_, bf16[2,8,128,512]{3,2,1,0:T(8,128)(2,1)} %refs_2_.5, bf16[2,128,512]{2,1,0:T(8,128)(2,1)} %copy-done.1, bf16[2,128,512]{2,1,0:T(8,128)(2,1)} %copy-done.2, ...), custom_call_target="tpu_custom_call" | custom-call | tf_op jit(solution)/shard_map/pallas_call | solution.py:423
  96.8 0.7 collective-permute-start.13
  97.7 0.5 copy-done.6
  98.2 15.9 %shard_map.65 = (f32[1,2,512,512]{3,2,1,0:T(8,128)}, bf16[2,8,128,512]{3,2,1,0:T(8,128)(2,1)}) custom-call(s32[4]{0:T(128)} %refs_0_.5, s32[3]{0:T(128)} %pad_add_fusion.place.refs_1_, bf16[2,8,128,512]{3,2,1,0:T(8,128)(2,1)} %refs_2_.5, bf16[2,128,512]{2,1,0:T(8,128)(2,1)} %copy-done.1, bf16[2,128,512]{2,1,0:T(8,128)(2,1)} %copy-done.2, ...), custom_call_target="tpu_custom_call" | custom-call | tf_op jit(solution)/shard_map/pallas_call | solution.py:423
  114.1 0.9 copy-done.5
  115.1 9.1 %shard_map.66 = bf16[2,8,128,512]{3,2,1,0:T(8,128)(2,1)} custom-call(s32[4]{0:T(128)} %refs_0_.5, s32[3]{0:T(128)} %pad_add_fusion.place.refs_1_, bf16[2,8,128,512]{3,2,1,0:T(8,128)(2,1)} %refs_2_.5, bf16[2,128,512]{2,1,0:T(8,128)(2,1)} %copy-done.1, bf16[2,128,512]{2,1,0:T(8,128)(2,1)} %copy-done.2, ...), custom_call_target="tpu_custom_call", output_to_operand_aliasing={{}: (14, {})} | custom-call | tf_op jit(solution)/shard_map/pallas_call | solution.py:423
  (37 shorter events, 0.5 us)
Async XLA Ops:
  0.0 5.1 %copy-start = (bf16[2,8,128,512]{3,2,1,0:T(8,128)(2,1)S(1)}, bf16[2,8,128,512]{3,2,1,0:T(8,128)(2,1)}, u32[]{:S(2)}) copy-start(bf16[2,8,128,512]{3,2,1,0:T(8,128)(2,1)} %refs_2_.5) | copy-start | bytes 6291460
  4.4 1.8 %copy-start.8 = (f32[8,128]{1,0:T(8,128)S(1)}, f32[8,128]{1,0:T(8,128)}, u32[]{:S(2)}) copy-start(f32[8,128]{1,0:T(8,128)} %local_stats.1) | copy-start | bytes 12292
  4.4 1.8 %collective-permute-start = (f32[8,128]{1,0:T(8,128)}, f32[8,128]{1,0:T(8,128)S(1)}, u32[]{:S(2)}, u32[]{:S(2)}) collective-permute-start(f32[8,128]{1,0:T(8,128)} %local_stats.1), channel_id=1, source_target_pairs={{0,4},{4,0},{8,12},{12,8},{16,20},{20,16},{24,28},{28,24},{1,5},{5... | collective-permute-start | bytes 12296 | tf_op jit(solution)/shard_map/ppermute | solution.py:464
  6.3 5.4 %collective-permute-start.1 = (f32[8,128]{1,0:T(8,128)S(1)}, f32[8,128]{1,0:T(8,128)S(1)}, u32[]{:S(2)}, u32[]{:S(2)}) collective-permute-start(f32[8,128]{1,0:T(8,128)S(1)} %add.35), channel_id=1, source_target_pairs={{0,8},{4,12},{8,0},{12,4},{16,24},{20,28},{24,16},{28,20},{1,9},{5... | collective-permute-start | bytes 12296 | tf_op jit(solution)/shard_map/ppermute | solution.py:464
  8.3 63.3 %collective-permute-start.6 = (bf16[5,128,512]{2,1,0:T(8,128)(2,1)}, bf16[5,128,512]{2,1,0:T(8,128)(2,1)S(1)}, u32[]{:S(2)}, u32[]{:S(2)}) collective-permute-start(bf16[5,128,512]{2,1,0:T(8,128)(2,1)} %dynamic-slice_bitcast_fusion.1), channel_id=1, source_target_pairs={{0,1},{1,2},{2,3},{3,32},{32,33},{33,34},{34,35},{35,64},{64,65},{... | collective-permute-start | bytes 1966088 | tf_op jit(solution)/shard_map/ppermute | solution.py:473
  11.7 2.8 %collective-permute-start.2 = (f32[8,128]{1,0:T(8,128)S(1)}, f32[8,128]{1,0:T(8,128)S(1)}, u32[]{:S(2)}, u32[]{:S(2)}) collective-permute-start(f32[8,128]{1,0:T(8,128)S(1)} %add.36), channel_id=1, source_target_pairs={{0,24},{4,28},{8,16},{12,20},{16,8},{20,12},{24,0},{28,4},{1,25},{... | collective-permute-start | bytes 12296 | tf_op jit(solution)/shard_map/ppermute | solution.py:464
  14.6 7.9 %collective-permute-start.4 = (f32[8,128]{1,0:T(8,128)S(1)}, f32[8,128]{1,0:T(8,128)S(1)}, u32[]{:S(2)}, u32[]{:S(2)}) collective-permute-start(f32[8,128]{1,0:T(8,128)S(1)} %add.37), channel_id=1, source_target_pairs={{0,32},{32,0},{64,96},{96,64},{1,33},{33,1},{65,97},{97,65},{2,34}... | collective-permute-start | bytes 12296 | tf_op jit(solution)/shard_map/ppermute | solution.py:464
  16.2 8.9 %collective-permute-start.3 = (bf16[2,128,512]{2,1,0:T(8,128)(2,1)}, bf16[2,128,512]{2,1,0:T(8,128)(2,1)S(1)}, u32[]{:S(2)}, u32[]{:S(2)}) collective-permute-start(bf16[2,128,512]{2,1,0:T(8,128)(2,1)} %get-tuple-element.15), channel_id=1, source_target_pairs={{0,4},{4,8},{8,12},{12,16},{16,20},{20,24},{24,28},{1,5},{5,9},{9,... | collective-permute-start | bytes 786440 | tf_op jit(solution)/shard_map/ppermute | solution.py:478
  22.5 7.9 %collective-permute-start.5 = (bf16[2,128,512]{2,1,0:T(8,128)(2,1)}, bf16[2,128,512]{2,1,0:T(8,128)(2,1)S(1)}, u32[]{:S(2)}, u32[]{:S(2)}) collective-permute-start(bf16[2,128,512]{2,1,0:T(8,128)(2,1)} %get-tuple-element.16), channel_id=1, source_target_pairs={{4,0},{8,4},{12,8},{16,12},{20,16},{24,20},{28,24},{5,1},{9,5},{13... | collective-permute-start | bytes 786440 | tf_op jit(solution)/shard_map/ppermute | solution.py:480
  25.1 9.9 %copy-start.1 = (bf16[2,128,512]{2,1,0:T(8,128)(2,1)}, bf16[2,128,512]{2,1,0:T(8,128)(2,1)S(1)}, u32[]{:S(2)}) copy-start(bf16[2,128,512]{2,1,0:T(8,128)(2,1)S(1)} %collective-permute-done.3.refs_3_) | copy-start | bytes 786436
  30.4 4.6 %copy-start.2 = (bf16[2,128,512]{2,1,0:T(8,128)(2,1)}, bf16[2,128,512]{2,1,0:T(8,128)(2,1)S(1)}, u32[]{:S(2)}) copy-start(bf16[2,128,512]{2,1,0:T(8,128)(2,1)S(1)} %collective-permute-done.5.refs_4_) | copy-start | bytes 786436
  31.8 65.0 %collective-permute-start.9 = (bf16[6,128,512]{2,1,0:T(8,128)(2,1)S(1)}, bf16[6,128,512]{2,1,0:T(8,128)(2,1)S(1)}, u32[]{:S(2)}, u32[]{:S(2)}) collective-permute-start(bf16[6,128,512]{2,1,0:T(8,128)(2,1)S(1)} %maximum_select_fusion), channel_id=1, source_target_pairs={{0,1},{1,2},{2,3},{3,32},{32,33},{33,34},{34,35},{35,64},{64,65},{... | collective-permute-start | bytes 2359304 | tf_op jit(solution)/shard_map/ppermute | solution.py:494
  35.0 79.1 %collective-permute-start.12 = (bf16[7,128,512]{2,1,0:T(8,128)(2,1)S(1)}, bf16[7,128,512]{2,1,0:T(8,128)(2,1)S(1)}, u32[]{:S(2)}, u32[]{:S(2)}) collective-permute-start(bf16[7,128,512]{2,1,0:T(8,128)(2,1)S(1)} %dynamic-slice_bitcast_fusion), channel_id=1, source_target_pairs={{0,1},{1,2},{2,3},{3,32},{32,33},{33,34},{34,35},{35,64},{64,65},{... | collective-permute-start | bytes 2752520 | tf_op jit(solution)/shard_map/ppermute | solution.py:495
  37.5 3.7 %collective-permute-start.7 = (f32[8,128]{1,0:T(8,128)S(1)}, f32[8,128]{1,0:T(8,128)S(1)}, u32[]{:S(2)}, u32[]{:S(2)}) collective-permute-start(f32[8,128]{1,0:T(8,128)S(1)} %add.38), channel_id=1, source_target_pairs={{0,96},{32,64},{64,32},{96,0},{1,97},{33,65},{65,33},{97,1},{2,98}... | collective-permute-start | bytes 12296 | tf_op jit(solution)/shard_map/ppermute | solution.py:464
  41.3 30.3 %collective-permute-start.8 = (f32[8,128]{1,0:T(8,128)S(1)}, f32[8,128]{1,0:T(8,128)S(1)}, u32[]{:S(2)}, u32[]{:S(2)}) collective-permute-start(f32[8,128]{1,0:T(8,128)S(1)} %add.41), channel_id=1, source_target_pairs={{0,1},{1,0},{2,3},{3,2},{4,5},{5,4},{6,7},{7,6},{8,9},{9,8},{10,11... | collective-permute-start | bytes 12296 | tf_op jit(solution)/shard_map/ppermute | solution.py:482
  71.6 25.2 %copy-start.3 = (bf16[5,128,512]{2,1,0:T(8,128)(2,1)}, bf16[5,128,512]{2,1,0:T(8,128)(2,1)S(1)}, u32[]{:S(2)}) copy-start(bf16[5,128,512]{2,1,0:T(8,128)(2,1)S(1)} %collective-permute-done.6.refs_5_) | copy-start | bytes 1966084
  71.6 4.1 %collective-permute-start.10 = (f32[8,128]{1,0:T(8,128)S(1)}, f32[8,128]{1,0:T(8,128)S(1)}, u32[]{:S(2)}, u32[]{:S(2)}) collective-permute-start(f32[8,128]{1,0:T(8,128)S(1)} %add.42), channel_id=1, source_target_pairs={{0,3},{1,2},{2,1},{3,0},{4,7},{5,6},{6,5},{7,4},{8,11},{9,10},{10,... | collective-permute-start | bytes 12296 | tf_op jit(solution)/shard_map/ppermute | solution.py:493
  71.7 25.8 %collective-permute-start.11 = (bf16[1,128,512]{2,1,0:T(8,128)(2,1)S(1)}, bf16[1,128,512]{2,1,0:T(8,128)(2,1)S(1)}, u32[]{:S(2)}, u32[]{:S(2)}) collective-permute-start(bf16[1,128,512]{2,1,0:T(8,128)(2,1)S(1)} %slice_select_fusion), channel_id=1, source_target_pairs={{0,4},{4,0},{8,12},{12,8},{16,20},{20,16},{24,28},{28,24},{1,5},{5... | collective-permute-start | bytes 393224 | tf_op jit(solution)/shard_map/ppermute | solution.py:492
  96.8 0.9 copy-start.4
  96.8 17.3 %collective-permute-start.13 = (bf16[1,128,512]{2,1,0:T(8,128)(2,1)S(1)}, bf16[1,128,512]{2,1,0:T(8,128)(2,1)S(1)}, u32[]{:S(2)}, u32[]{:S(2)}) collective-permute-start(bf16[1,128,512]{2,1,0:T(8,128)(2,1)S(1)} %slice.59), channel_id=1, source_target_pairs={{0,4},{4,0},{8,12},{12,8},{16,20},{20,16},{24,28},{28,24},{1,5},{5... | collective-permute-start | bytes 393224 | tf_op jit(solution)/shard_map/ppermute | solution.py:506
  97.5 0.6 copy-start.6
  114.1 1.0 copy-start.5
  114.1 1.0 copy-start.7
where the time goes:
time: 125 us; the launch traced here: 124 us
  Pallas kernels  49.4 us (40%)
  waiting for transfers between devices  44.5 us (36%)
  starting transfers between devices  20.6 us (16%)
  local copies, waits for them, and re-layouts  6.81 us (5%)
  other arithmetic  2.66 us (2%)
    pallas_call x3, Pallas kernels, conv_stage(): pl.pallas_call(functools.partial(conv_kernel, stage, cells_per_frame, per...  45.5 us
    ppermute x1, waiting for transfers between devices, shards(): other = lax.ppermute(total, 'span', ring(0))  29.4 us
    ppermute x5, waiting for transfers between devices, fold(): return value + lax.ppermute(value, axis, partner)  5.46 us
    ppermute x1, starting transfers between devices, shards(): top = lax.ppermute(after(latents[:, -1], total), 'tile', down)  5.28 us
    ppermute x1, waiting for transfers between devices, shards(): bottom = lax.ppermute(after(latents[:, 0], total), 'tile', up)  5.23 us
    pallas_call x1, Pallas kernels, local_stats(): pl.pallas_call(functools.partial(stats_kernel, per_group, frames), grid_s...  3.82 us
    ppermute x1, waiting for transfers between devices, shards(): other = lax.ppermute(total, 'span', ring(1))  3.68 us
    ppermute x5, starting transfers between devices, fold(): return value + lax.ppermute(value, axis, partner)  3.66 us
  transfers between devices with their start and end apart: 14, of which 6 were waited for; matrix products, arithmetic and copies ran while one was open for 6% of the time, Pallas kernels for 29%

commit v1 on v0

--- a/solution.py
+++ b/solution.py
@@ -9,7 +9,7 @@
 
 GROUPS = 32
 EPSILON = 1e-06
-EARLY = 5
+EARLY = 6
 LANES = 128
 HIGHEST = lax.Precision.HIGHEST
 
@@ -479,14 +479,13 @@
     total = fold(total, "req", ring(0))
     bottom = lax.ppermute(after(latents[:, 0], total), "tile", up)
     total = fold(total, "req", ring(1))
-    other = lax.ppermute(total, "span", ring(0))
+    total = fold(total, "span", ring(0))
     pair_send = jnp.where(
         first_core,
         jnp.concatenate([top[1:], latents[1, :late], top[:1], latents[0, rows - 1 :]]),
         jnp.concatenate([latents[1, EARLY:], bottom[1:], bottom[:1], latents[0, :1]]),
     )
     far_send = lax.dynamic_slice_in_dim(latents[0], core, rows - 1, axis=0)
-    total = total + other
     near_rows, total = lax.optimization_barrier((near_rows, total))
     inner_send = jnp.where(first_core, near_rows[EARLY - 1], near_rows[0])[None]
     inner_1 = lax.ppermute(inner_send, "tile", swap)

time: 125 us -> 116 us (0.928)
  the two profiles are of different devices: /device:TPU:23 before, /device:TPU:41 now
where the time goes in v1:
time: 116 us; the launch traced here: 115 us
  Pallas kernels  48.9 us (42%)
  starting transfers between devices  28.9 us (25%)
  waiting for transfers between devices  26.2 us (23%)
  local copies, waits for them, and re-layouts  8.07 us (7%)
  other arithmetic  2.58 us (2%)
    pallas_call x3, Pallas kernels, conv_stage(): pl.pallas_call(functools.partial(conv_kernel, stage, cells_per_frame, per...  45.1 us
    ppermute x6, waiting for transfers between devices, fold(): return value + lax.ppermute(value, axis, partner)  20.5 us
    ppermute x6, starting transfers between devices, fold(): return value + lax.ppermute(value, axis, partner)  6.75 us
    ppermute x1, waiting for transfers between devices, shards(): bottom = lax.ppermute(after(latents[:, 0], total), 'tile', up)  5.53 us
    ppermute x1, starting transfers between devices, shards(): top = lax.ppermute(after(latents[:, -1], total), 'tile', down)  5.52 us
    pallas_call x1, Pallas kernels, local_stats(): pl.pallas_call(functools.partial(stats_kernel, per_group, frames), grid_s...  3.82 us
    ppermute x1, starting transfers between devices, shards(): other = lax.ppermute(total, 'span', ring(1))  3.55 us
    ppermute x1, starting transfers between devices, shards(): far_rows = lax.ppermute(far_send, spread, onward)  3.11 us
  transfers between devices with their start and end apart: 14, of which 5 were waited for; matrix products, arithmetic and copies ran while one was open for 8% of the time, Pallas kernels for 31%

profile of v1, /device:TPU:41, one launch (start us, length us, event | category | flops | bytes accessed | tf_op | source)
XLA Modules:
  0.0 115.1 jit_solution(16583093768612495238)
XLA Ops:
  0.0 0.6 pad_add_fusion.place.refs_1_
  0.6 3.8 %local_stats.1 = f32[8,128]{1,0:T(8,128)} custom-call(s32[4]{0:T(128)} %refs_0_.5, s32[3]{0:T(128)} %pad_add_fusion.place.refs_1_, bf16[2,8,128,512]{3,2,1,0:T(8,128)(2,1)} %refs_2_.5), custom_call_target="tpu_custom_call" | custom-call | tf_op jit(solution)/shard_map/local_stats/pallas_call | solution.py:89
  4.4 0.7 collective-permute-start
  5.1 1.2 %fusion = (bf16[1,8,128,512]{3,2,1,0:T(8,128)(2,1)}, bf16[1,8,128,512]{3,2,1,0:T(8,128)(2,1)S(1)}) fusion(bf16[2,8,128,512]{3,2,1,0:T(8,128)(2,1)S(1)} %copy-done), kind=kLoop, calls=%fused_computation.11 | loop fusion | bytes 4194304 | tf_op jit(solution)/shard_map/slice | solution.py:488
  6.3 0.9 dynamic-slice_bitcast_fusion.1
  7.2 3.1 %collective-permute-start.6 = (bf16[6,128,512]{2,1,0:T(8,128)(2,1)}, bf16[6,128,512]{2,1,0:T(8,128)(2,1)S(1)}, u32[]{:S(2)}, u32[]{:S(2)}) collective-permute-start(bf16[6,128,512]{2,1,0:T(8,128)(2,1)} %dynamic-slice_bitcast_fusion.1), channel_id=1, source_target_pairs={{0,1},{1,2},{2,3},{3,32},{32,33},{33,34},{34,35},{35,64},{64,65},{... | collective-permute-start | bytes 2359304 | tf_op jit(solution)/shard_map/ppermute | solution.py:473
  10.4 0.2 collective-permute-start.1
  10.6 2.2 %dynamic-slice_bitcast_fusion = bf16[7,128,512]{2,1,0:T(8,128)(2,1)} fusion(bf16[1,8,128,512]{3,2,1,0:T(8,128)(2,1)} %get-tuple-element.25, s32[]{:T(128)S(6)} %select_n.36), kind=kLoop, calls=%fused_computation | loop fusion | bytes 1835012 | tf_op jit(solution)/shard_map/dynamic_slice | solution.py:488
  12.9 3.1 %collective-permute-start.12 = (bf16[7,128,512]{2,1,0:T(8,128)(2,1)}, bf16[7,128,512]{2,1,0:T(8,128)(2,1)}, u32[]{:S(2)}, u32[]{:S(2)}) collective-permute-start(bf16[7,128,512]{2,1,0:T(8,128)(2,1)} %dynamic-slice_bitcast_fusion), channel_id=1, source_target_pairs={{0,1},{1,2},{2,3},{3,32},{32,33},{33,34},{34,35},{35,64},{64,65},{... | collective-permute-start | bytes 2752520 | tf_op jit(solution)/shard_map/ppermute | solution.py:494
  16.0 2.2 %collective-permute-start.2 = (f32[8,128]{1,0:T(8,128)S(1)}, f32[8,128]{1,0:T(8,128)S(1)}, u32[]{:S(2)}, u32[]{:S(2)}) collective-permute-start(f32[8,128]{1,0:T(8,128)S(1)} %add.36), channel_id=1, source_target_pairs={{0,24},{4,28},{8,16},{12,20},{16,8},{20,12},{24,0},{28,4},{1,25},{... | collective-permute-start | bytes 12296 | tf_op jit(solution)/shard_map/ppermute | solution.py:464
  18.2 0.8 slice_bitcast_fusion.2
  19.0 0.5 collective-permute-done.2
  19.5 0.4 collective-permute-start.4
  19.9 5.5 %collective-permute-start.3 = (bf16[2,128,512]{2,1,0:T(8,128)(2,1)}, bf16[2,128,512]{2,1,0:T(8,128)(2,1)S(1)}, u32[]{:S(2)}, u32[]{:S(2)}) collective-permute-start(bf16[2,128,512]{2,1,0:T(8,128)(2,1)} %get-tuple-element.15), channel_id=1, source_target_pairs={{0,4},{4,8},{8,12},{12,16},{16,20},{20,24},{24,28},{1,5},{5,9},{9,... | collective-permute-start | bytes 786440 | tf_op jit(solution)/shard_map/ppermute | solution.py:478
  25.4 0.9 slice_bitcast_fusion
  26.3 1.9 %collective-permute-start.5 = (bf16[2,128,512]{2,1,0:T(8,128)(2,1)}, bf16[2,128,512]{2,1,0:T(8,128)(2,1)S(1)}, u32[]{:S(2)}, u32[]{:S(2)}) collective-permute-start(bf16[2,128,512]{2,1,0:T(8,128)(2,1)} %get-tuple-element.16), channel_id=1, source_target_pairs={{4,0},{8,4},{12,8},{16,12},{20,16},{24,20},{28,24},{5,1},{9,5},{13... | collective-permute-start | bytes 786440 | tf_op jit(solution)/shard_map/ppermute | solution.py:480
  28.2 0.7 slice_bitcast_fusion.4
  29.0 5.5 %collective-permute-done.5.refs_4_ = bf16[2,128,512]{2,1,0:T(8,128)(2,1)S(1)} collective-permute-done((bf16[2,128,512]{2,1,0:T(8,128)(2,1)}, bf16[2,128,512]{2,1,0:T(8,128)(2,1)S(1)}, u32[]{:S(2)}, u32[]{:S(2)}) %collective-permute-start.5) | collective-permute-done | bytes 262176 | tf_op jit(solution)/shard_map/ppermute | solution.py:480
  34.6 1.3 %maximum_select_fusion = bf16[5,128,512]{2,1,0:T(8,128)(2,1)S(1)} fusion(bf16[1,128,512]{2,1,0:T(8,128)(2,1)} %get-tuple-element.30, bf16[1,128,512]{2,1,0:T(8,128)(2,1)S(1)} %get-tuple-element.36, bf16[2,128,512]{2,1,0:T(8,128)(2,1)} %get-tuple-element.28, bf16[1,128,512]{2,1,0:T(8,128)(2,1)S(1)} %get-tuple-element.35, ...), kind=kLoop, calls=%fused_computation.2 | loop fusion | flops 2293760 | bytes 1966081 | tf_op jit(solution)/shard_map/jit(_where)/select_n | solution.py:483
  35.9 2.0 %collective-permute-start.9 = (bf16[5,128,512]{2,1,0:T(8,128)(2,1)S(1)}, bf16[5,128,512]{2,1,0:T(8,128)(2,1)S(1)}, u32[]{:S(2)}, u32[]{:S(2)}) collective-permute-start(bf16[5,128,512]{2,1,0:T(8,128)(2,1)S(1)} %maximum_select_fusion), channel_id=1, source_target_pairs={{0,1},{1,2},{2,3},{3,32},{32,33},{33,34},{34,35},{35,64},{64,65},{... | collective-permute-start | bytes 1966088 | tf_op jit(solution)/shard_map/ppermute | solution.py:493
  37.9 3.2 %collective-permute-start.7 = (f32[8,128]{1,0:T(8,128)S(1)}, f32[8,128]{1,0:T(8,128)S(1)}, u32[]{:S(2)}, u32[]{:S(2)}) collective-permute-start(f32[8,128]{1,0:T(8,128)S(1)} %add.38), channel_id=1, source_target_pairs={{0,96},{32,64},{64,32},{96,0},{1,97},{33,65},{65,33},{97,1},{2,98}... | collective-permute-start | bytes 12296 | tf_op jit(solution)/shard_map/ppermute | solution.py:464
  41.2 1.4 %collective-permute-done.7 = f32[8,128]{1,0:T(8,128)S(1)} collective-permute-done((f32[8,128]{1,0:T(8,128)S(1)}, f32[8,128]{1,0:T(8,128)S(1)}, u32[]{:S(2)}, u32[]{:S(2)}) %collective-permute-start.7) | collective-permute-done | bytes 4128 | tf_op jit(solution)/shard_map/ppermute | solution.py:464
  42.6 18.6 %collective-permute-done.8 = f32[8,128]{1,0:T(8,128)S(1)} collective-permute-done((f32[8,128]{1,0:T(8,128)S(1)}, f32[8,128]{1,0:T(8,128)S(1)}, u32[]{:S(2)}, u32[]{:S(2)}) %collective-permute-start.8) | collective-permute-done | bytes 4128 | tf_op jit(solution)/shard_map/ppermute | solution.py:464
  61.2 3.5 %collective-permute-start.10 = (f32[8,128]{1,0:T(8,128)S(1)}, f32[8,128]{1,0:T(8,128)S(1)}, u32[]{:S(2)}, u32[]{:S(2)}) collective-permute-start(f32[8,128]{1,0:T(8,128)S(1)} %add.42), channel_id=1, source_target_pairs={{0,3},{1,2},{2,1},{3,0},{4,7},{5,6},{6,5},{7,4},{8,11},{9,10},{10,... | collective-permute-start | bytes 12296 | tf_op jit(solution)/shard_map/ppermute | solution.py:492
  64.8 1.4 %collective-permute-start.11 = (bf16[1,128,512]{2,1,0:T(8,128)(2,1)S(1)}, bf16[1,128,512]{2,1,0:T(8,128)(2,1)S(1)}, u32[]{:S(2)}, u32[]{:S(2)}) collective-permute-start(bf16[1,128,512]{2,1,0:T(8,128)(2,1)S(1)} %slice_select_fusion), channel_id=1, source_target_pairs={{0,4},{4,0},{8,12},{12,8},{16,20},{20,16},{24,28},{28,24},{1,5},{5... | collective-permute-start | bytes 393224 | tf_op jit(solution)/shard_map/ppermute | solution.py:491
  66.2 0.6 add.43.refs_6_
  66.8 20.5 %shard_map.64 = (f32[8,512]{1,0:T(8,128)}, f32[2,2,512,512]{3,2,1,0:T(8,128)}) custom-call(s32[4]{0:T(128)} %refs_0_.5, s32[3]{0:T(128)} %pad_add_fusion.place.refs_1_, bf16[2,8,128,512]{3,2,1,0:T(8,128)(2,1)} %refs_2_.5, bf16[2,128,512]{2,1,0:T(8,128)(2,1)} %copy-done.2, bf16[2,128,512]{2,1,0:T(8,128)(2,1)} %copy-done.3, ...), custom_call_target="tpu_custom_call" | custom-call | tf_op jit(solution)/shard_map/pallas_call | solution.py:423
  87.4 1.6 %collective-permute-start.13 = (bf16[1,128,512]{2,1,0:T(8,128)(2,1)S(1)}, bf16[1,128,512]{2,1,0:T(8,128)(2,1)S(1)}, u32[]{:S(2)}, u32[]{:S(2)}) collective-permute-start(bf16[1,128,512]{2,1,0:T(8,128)(2,1)S(1)} %slice.59), channel_id=1, source_target_pairs={{0,4},{4,0},{8,12},{12,8},{16,20},{20,16},{24,28},{28,24},{1,5},{5... | collective-permute-start | bytes 393224 | tf_op jit(solution)/shard_map/ppermute | solution.py:505
  89.0 0.7 copy-done.5
  89.6 15.5 %shard_map.65 = (f32[1,2,512,512]{3,2,1,0:T(8,128)}, bf16[2,8,128,512]{3,2,1,0:T(8,128)(2,1)}) custom-call(s32[4]{0:T(128)} %refs_0_.5, s32[3]{0:T(128)} %pad_add_fusion.place.refs_1_, bf16[2,8,128,512]{3,2,1,0:T(8,128)(2,1)} %refs_2_.5, bf16[2,128,512]{2,1,0:T(8,128)(2,1)} %copy-done.2, bf16[2,128,512]{2,1,0:T(8,128)(2,1)} %copy-done.3, ...), custom_call_target="tpu_custom_call" | custom-call | tf_op jit(solution)/shard_map/pallas_call | solution.py:423
  105.2 0.6 copy-done.6
  105.8 9.1 %shard_map.66 = bf16[2,8,128,512]{3,2,1,0:T(8,128)(2,1)} custom-call(s32[4]{0:T(128)} %refs_0_.5, s32[3]{0:T(128)} %pad_add_fusion.place.refs_1_, bf16[2,8,128,512]{3,2,1,0:T(8,128)(2,1)} %refs_2_.5, bf16[2,128,512]{2,1,0:T(8,128)(2,1)} %copy-done.2, bf16[2,128,512]{2,1,0:T(8,128)(2,1)} %copy-done.3, ...), custom_call_target="tpu_custom_call", output_to_operand_aliasing={{}: (14, {})} | custom-call | tf_op jit(solution)/shard_map/pallas_call | solution.py:423
  (35 shorter events, 0.3 us)
Async XLA Ops:
  0.0 5.1 %copy-start = (bf16[2,8,128,512]{3,2,1,0:T(8,128)(2,1)S(1)}, bf16[2,8,128,512]{3,2,1,0:T(8,128)(2,1)}, u32[]{:S(2)}) copy-start(bf16[2,8,128,512]{3,2,1,0:T(8,128)(2,1)} %refs_2_.5) | copy-start | bytes 6291460
  4.4 5.9 %collective-permute-start = (f32[8,128]{1,0:T(8,128)}, f32[8,128]{1,0:T(8,128)S(1)}, u32[]{:S(2)}, u32[]{:S(2)}) collective-permute-start(f32[8,128]{1,0:T(8,128)} %local_stats.1), channel_id=1, source_target_pairs={{0,4},{4,0},{8,12},{12,8},{16,20},{20,16},{24,28},{28,24},{1,5},{5... | collective-permute-start | bytes 12296 | tf_op jit(solution)/shard_map/ppermute | solution.py:464
  5.1 5.2 %copy-start.7 = (f32[8,128]{1,0:T(8,128)S(1)}, f32[8,128]{1,0:T(8,128)}, u32[]{:S(2)}) copy-start(f32[8,128]{1,0:T(8,128)} %local_stats.1) | copy-start | bytes 12292
  7.2 54.0 %collective-permute-start.6 = (bf16[6,128,512]{2,1,0:T(8,128)(2,1)}, bf16[6,128,512]{2,1,0:T(8,128)(2,1)S(1)}, u32[]{:S(2)}, u32[]{:S(2)}) collective-permute-start(bf16[6,128,512]{2,1,0:T(8,128)(2,1)} %dynamic-slice_bitcast_fusion.1), channel_id=1, source_target_pairs={{0,1},{1,2},{2,3},{3,32},{32,33},{33,34},{34,35},{35,64},{64,65},{... | collective-permute-start | bytes 2359304 | tf_op jit(solution)/shard_map/ppermute | solution.py:473
  10.4 5.6 %collective-permute-start.1 = (f32[8,128]{1,0:T(8,128)S(1)}, f32[8,128]{1,0:T(8,128)S(1)}, u32[]{:S(2)}, u32[]{:S(2)}) collective-permute-start(f32[8,128]{1,0:T(8,128)S(1)} %add.35), channel_id=1, source_target_pairs={{0,8},{4,12},{8,0},{12,4},{16,24},{20,28},{24,16},{28,20},{1,9},{5... | collective-permute-start | bytes 12296 | tf_op jit(solution)/shard_map/ppermute | solution.py:464
  12.9 92.3 %collective-permute-start.12 = (bf16[7,128,512]{2,1,0:T(8,128)(2,1)}, bf16[7,128,512]{2,1,0:T(8,128)(2,1)}, u32[]{:S(2)}, u32[]{:S(2)}) collective-permute-start(bf16[7,128,512]{2,1,0:T(8,128)(2,1)} %dynamic-slice_bitcast_fusion), channel_id=1, source_target_pairs={{0,1},{1,2},{2,3},{3,32},{32,33},{33,34},{34,35},{35,64},{64,65},{... | collective-permute-start | bytes 2752520 | tf_op jit(solution)/shard_map/ppermute | solution.py:494
  16.0 3.5 %collective-permute-start.2 = (f32[8,128]{1,0:T(8,128)S(1)}, f32[8,128]{1,0:T(8,128)S(1)}, u32[]{:S(2)}, u32[]{:S(2)}) collective-permute-start(f32[8,128]{1,0:T(8,128)S(1)} %add.36), channel_id=1, source_target_pairs={{0,24},{4,28},{8,16},{12,20},{16,8},{20,12},{24,0},{28,4},{1,25},{... | collective-permute-start | bytes 12296 | tf_op jit(solution)/shard_map/ppermute | solution.py:464
  19.5 6.8 %collective-permute-start.4 = (f32[8,128]{1,0:T(8,128)S(1)}, f32[8,128]{1,0:T(8,128)S(1)}, u32[]{:S(2)}, u32[]{:S(2)}) collective-permute-start(f32[8,128]{1,0:T(8,128)S(1)} %add.37), channel_id=1, source_target_pairs={{0,32},{32,0},{64,96},{96,64},{1,33},{33,1},{65,97},{97,65},{2,34}... | collective-permute-start | bytes 12296 | tf_op jit(solution)/shard_map/ppermute | solution.py:464
  19.9 9.1 %collective-permute-start.3 = (bf16[2,128,512]{2,1,0:T(8,128)(2,1)}, bf16[2,128,512]{2,1,0:T(8,128)(2,1)S(1)}, u32[]{:S(2)}, u32[]{:S(2)}) collective-permute-start(bf16[2,128,512]{2,1,0:T(8,128)(2,1)} %get-tuple-element.15), channel_id=1, source_target_pairs={{0,4},{4,8},{8,12},{12,16},{16,20},{20,24},{24,28},{1,5},{5,9},{9,... | collective-permute-start | bytes 786440 | tf_op jit(solution)/shard_map/ppermute | solution.py:478
  26.3 8.3 %collective-permute-start.5 = (bf16[2,128,512]{2,1,0:T(8,128)(2,1)}, bf16[2,128,512]{2,1,0:T(8,128)(2,1)S(1)}, u32[]{:S(2)}, u32[]{:S(2)}) collective-permute-start(bf16[2,128,512]{2,1,0:T(8,128)(2,1)} %get-tuple-element.16), channel_id=1, source_target_pairs={{4,0},{8,4},{12,8},{16,12},{20,16},{24,20},{28,24},{5,1},{9,5},{13... | collective-permute-start | bytes 786440 | tf_op jit(solution)/shard_map/ppermute | solution.py:480
  29.0 37.8 %copy-start.2 = (bf16[2,128,512]{2,1,0:T(8,128)(2,1)}, bf16[2,128,512]{2,1,0:T(8,128)(2,1)S(1)}, u32[]{:S(2)}) copy-start(bf16[2,128,512]{2,1,0:T(8,128)(2,1)S(1)} %collective-permute-done.3.refs_3_) | copy-start | bytes 786436
  34.6 32.2 %copy-start.3 = (bf16[2,128,512]{2,1,0:T(8,128)(2,1)}, bf16[2,128,512]{2,1,0:T(8,128)(2,1)S(1)}, u32[]{:S(2)}) copy-start(bf16[2,128,512]{2,1,0:T(8,128)(2,1)S(1)} %collective-permute-done.5.refs_4_) | copy-start | bytes 786436
  35.9 51.4 %collective-permute-start.9 = (bf16[5,128,512]{2,1,0:T(8,128)(2,1)S(1)}, bf16[5,128,512]{2,1,0:T(8,128)(2,1)S(1)}, u32[]{:S(2)}, u32[]{:S(2)}) collective-permute-start(bf16[5,128,512]{2,1,0:T(8,128)(2,1)S(1)} %maximum_select_fusion), channel_id=1, source_target_pairs={{0,1},{1,2},{2,3},{3,32},{32,33},{33,34},{34,35},{35,64},{64,65},{... | collective-permute-start | bytes 1966088 | tf_op jit(solution)/shard_map/ppermute | solution.py:493
  37.9 4.6 %collective-permute-start.7 = (f32[8,128]{1,0:T(8,128)S(1)}, f32[8,128]{1,0:T(8,128)S(1)}, u32[]{:S(2)}, u32[]{:S(2)}) collective-permute-start(f32[8,128]{1,0:T(8,128)S(1)} %add.38), channel_id=1, source_target_pairs={{0,96},{32,64},{64,32},{96,0},{1,97},{33,65},{65,33},{97,1},{2,98}... | collective-permute-start | bytes 12296 | tf_op jit(solution)/shard_map/ppermute | solution.py:464
  42.6 18.6 %collective-permute-start.8 = (f32[8,128]{1,0:T(8,128)S(1)}, f32[8,128]{1,0:T(8,128)S(1)}, u32[]{:S(2)}, u32[]{:S(2)}) collective-permute-start(f32[8,128]{1,0:T(8,128)S(1)} %add.41), channel_id=1, source_target_pairs={{0,1},{1,0},{2,3},{3,2},{4,5},{5,4},{6,7},{7,6},{8,9},{9,8},{10,11... | collective-permute-start | bytes 12296 | tf_op jit(solution)/shard_map/ppermute | solution.py:464
  61.2 26.1 %copy-start.1 = (bf16[6,128,512]{2,1,0:T(8,128)(2,1)}, bf16[6,128,512]{2,1,0:T(8,128)(2,1)S(1)}, u32[]{:S(2)}) copy-start(bf16[6,128,512]{2,1,0:T(8,128)(2,1)S(1)} %collective-permute-done.6.refs_5_) | copy-start | bytes 2359300
  61.2 5.0 %collective-permute-start.10 = (f32[8,128]{1,0:T(8,128)S(1)}, f32[8,128]{1,0:T(8,128)S(1)}, u32[]{:S(2)}, u32[]{:S(2)}) collective-permute-start(f32[8,128]{1,0:T(8,128)S(1)} %add.42), channel_id=1, source_target_pairs={{0,3},{1,2},{2,1},{3,0},{4,7},{5,6},{6,5},{7,4},{8,11},{9,10},{10,... | collective-permute-start | bytes 12296 | tf_op jit(solution)/shard_map/ppermute | solution.py:492
  64.8 24.2 %collective-permute-start.11 = (bf16[1,128,512]{2,1,0:T(8,128)(2,1)S(1)}, bf16[1,128,512]{2,1,0:T(8,128)(2,1)S(1)}, u32[]{:S(2)}, u32[]{:S(2)}) collective-permute-start(bf16[1,128,512]{2,1,0:T(8,128)(2,1)S(1)} %slice_select_fusion), channel_id=1, source_target_pairs={{0,4},{4,0},{8,12},{12,8},{16,20},{20,16},{24,28},{28,24},{1,5},{5... | collective-permute-start | bytes 393224 | tf_op jit(solution)/shard_map/ppermute | solution.py:491
  87.3 1.6 %copy-start.4 = (bf16[5,128,512]{2,1,0:T(8,128)(2,1)}, bf16[5,128,512]{2,1,0:T(8,128)(2,1)S(1)}, u32[]{:S(2)}) copy-start(bf16[5,128,512]{2,1,0:T(8,128)(2,1)S(1)} %collective-permute-done.9.refs_6_) | copy-start | bytes 1966084
  87.4 17.8 %collective-permute-start.13 = (bf16[1,128,512]{2,1,0:T(8,128)(2,1)S(1)}, bf16[1,128,512]{2,1,0:T(8,128)(2,1)S(1)}, u32[]{:S(2)}, u32[]{:S(2)}) collective-permute-start(bf16[1,128,512]{2,1,0:T(8,128)(2,1)S(1)} %slice.59), channel_id=1, source_target_pairs={{0,4},{4,0},{8,12},{12,8},{16,20},{20,16},{24,28},{28,24},{1,5},{5... | collective-permute-start | bytes 393224 | tf_op jit(solution)/shard_map/ppermute | solution.py:505
  89.0 0.7 copy-start.5
  105.2 0.6 copy-start.6
